TPU v7x, 512 devices: a whole 4x4x16 slice. The times are simulated.
512 devices in a mesh: seq: 32 (over z, core), heads: 4 (over x), dp: 4 (over y).
Axes of the slice: x: 4, y: 4, z: 16, core: 2. Of those that a mesh axis runs over, the one named last changes fastest.
Arguments:
- tokens: bfloat16 [4, 4096, 3072], P('dp', 'seq'), may hold values from -6 to 6
- proj_weights: bfloat16 [3, 3072, 4096], P(None, 'seq', ('heads', 'dp')), may hold values from -0.109375 to 0.109375
- norm_gain: float32 [4096], P(('heads', 'dp')), may hold values from 0.5 to 1.5
Outputs:
- attended: bfloat16 [4, 4096, 4096], P('dp', 'seq', 'heads')
All inputs are finite; a program needn't handle non-finite values.
Results may differ from a plain program's by a relative error of at most 0.0063.
Values may be sent and summed in bfloat16 or wider, within the bound.
No kernel may reach another device: no remote copies, remote signals or barrier semaphores. Data moves between devices by JAX's collectives and lax.ppermute only.
A program may use at most 64 MiB of HBM per device.

v0:
```python
import jax
import jax.numpy as jnp
from jax import lax
from jax.sharding import PartitionSpec as P

DH = 128


def prefix_2(part, axis, combine, identity):
    place = lax.axis_index(axis)
    gathered = lax.all_gather(part, axis)
    state = jnp.zeros_like(part) + jnp.asarray(identity, part.dtype)

    def one(step, state):
        return combine(state, lax.dynamic_index_in_dim(gathered, step, 0, False))

    return lax.fori_loop(0, place, one, state)


def add_pair(earlier, later):
    return earlier + later


def project_rows(flat_rows):

    def accumulate(total, piece, start):
        return jnp.einsum("nd,jdc->jnc", flat_rows, piece, preferred_element_type=jnp.float32)

    return accumulate


def to_heads(matrix, seq_count, length):
    return matrix.reshape(seq_count, length, -1, DH)


def activate(matrix, seq_count, length):
    return to_heads(jax.nn.silu(matrix).astype(jnp.bfloat16), seq_count, length)


def block_prefix(keys_b, values_b):
    state = jnp.einsum("sthd,sthe->shde", keys_b, values_b, preferred_element_type=jnp.float32)
    return prefix_2(state, "seq", add_pair, jnp.zeros_like(state))


def attend(queries, keys_b, values_b, prefix, norm_gain):
    seq_count, length, head_count, head_size = queries.shape
    scores = jnp.einsum("sthd,suhd->shtu", queries, keys_b, preferred_element_type=jnp.float32)
    causal = lax.broadcasted_iota(jnp.int32, (length, length), 0) >= lax.broadcasted_iota(
        jnp.int32, (length, length), 1
    )
    scores_b = jnp.where(causal, scores, 0.0).astype(jnp.bfloat16)
    local = jnp.einsum("shtu,suhd->sthd", scores_b, values_b, preferred_element_type=jnp.float32)
    carried = jnp.einsum(
        "sthd,shde->sthe", queries, prefix.astype(jnp.bfloat16), preferred_element_type=jnp.float32
    )
    attn = local + carried
    scale = lax.rsqrt(jnp.mean(attn * attn, axis=-1, keepdims=True) + 1e-06)
    normed = attn * scale * norm_gain.reshape(head_count, head_size)
    return normed.astype(jnp.bfloat16).reshape(seq_count, length, head_count * head_size)


def body(tokens, proj_weights, norm_gain):
    everyone = lax.all_gather(tokens, "dp", axis=0, tiled=True)
    seq_count, length, width = everyone.shape
    total_rows = seq_count * length
    per_device = proj_weights.shape[2]
    accumulate = project_rows(everyone.reshape(total_rows, width))
    start_sum = jnp.zeros((3, total_rows, per_device), jnp.float32)
    projected = accumulate(
        start_sum, lax.all_gather(proj_weights, "seq", axis=1, tiled=True), jnp.int32(0)
    )
    queries = activate(projected[0], seq_count, length)
    keys_b = activate(projected[1], seq_count, length)
    values_b = to_heads(projected[2].astype(jnp.bfloat16), seq_count, length)
    prefix = block_prefix(keys_b, values_b)
    normed = attend(queries, keys_b, values_b, prefix, norm_gain)
    return lax.all_to_all(normed, "dp", split_axis=0, concat_axis=2, tiled=True)


def solution(mesh):
    in_specs = (P("dp", "seq", None), P(None, "seq", ("heads", "dp")), P(("heads", "dp")))
    out_specs = P("dp", "seq", "heads")
    return jax.shard_map(body, mesh=mesh, in_specs=in_specs, out_specs=out_specs, check_vma=False)
```

profile of v0, /device:TPU:481, one launch (start us, length us, event | category | flops | bytes accessed | tf_op | source)
XLA Modules:
  0.0 297.7 jit_solution(694654217346947341)
XLA Ops:
  8.1 47.7 %all-gather.7.cloned.1.call-done = bf16[4,128,3072]{2,1,0:T(8,128)(2,1)} async-done(((bf16[1,128,3072]{2,1,0:T(8,128)(2,1)}), bf16[4,128,3072]{2,1,0:T(8,128)(2,1)}) %all-gather.7.cloned.1.call-update) | async-done | bytes 3145744 | tf_op jit(solution)/shard_map/all_gather | solution.py:63
  55.8 76.4 %all-gather.5.cloned.1.call-done = bf16[3,3072,256]{2,1,0:T(8,128)(2,1)} async-done(((bf16[3,96,256]{2,1,0:T(8,128)(2,1)}), bf16[3,3072,256]{2,1,0:T(8,128)(2,1)}) %all-gather.5.cloned.1.call-update) | async-done | bytes 4718608 | tf_op jit(solution)/shard_map/all_gather | solution.py:70
  132.1 5.5 %convolution_bitcast_fusion = f32[3,512,256]{1,2,0:T(8,128)S(1)} fusion(bf16[3,3072,256]{2,1,0:T(8,128)(2,1)} %all-gather.5.cloned.1.call-done, bf16[512,3072,1]{1,0,2:T(8,128)(2,1)} %bitcast.33), kind=kOutput, calls=%fused_computation.1 | convolution fusion | flops 2415919104 | bytes 9437184 | tf_op jit(solution)/shard_map/nd,jdc->jnc/dot_general | solution.py:27
  140.6 101.5 %all-gather.9.cloned.1.call-done = f32[128,2,128,128]{3,2,1,0:T(8,128)} async-done(((f32[4,2,128,128]{3,2,1,0:T(8,128)}), f32[128,2,128,128]{3,2,1,0:T(8,128)}) %all-gather.9.cloned.1.call-update) | async-done | bytes 16777232 | tf_op jit(solution)/shard_map/all_gather | solution.py:11
  242.2 37.0 %while.10 = (s32[]{:T(128)}, f32[4,2,128,128]{3,2,1,0:T(8,128)S(1)}, s32[]{:T(128)}, f32[32,4,2,128,128]{4,3,2,1,0:T(8,128)}, s32[]{:T(128)}, /*index=5*/s32[]{:T(128)}, s32[]{:T(128)}) while((s32[]{:T(128)}, f32[4,2,128,128]{3,2,1,0:T(8,128)S(1)}, s32[]{:T(128)}, f32[32,4,2,128,128]{4,3,2,1,0:T(8,128)}, s32[]{:T(128)}, /*index=5*/s32[]{:T(128)}, ...), condition=%wide.region_1.2_spmd, body=%wide.region_0.1_spmd.sunk | while | flops 131077 | bytes 1572987 | solution.py:17
  242.2 1.2 bitcast_add_fusion.2
  243.4 1.2 bitcast_add_fusion.2
  244.6 1.2 bitcast_add_fusion.2
  245.8 1.2 bitcast_add_fusion.2
  247.0 1.2 bitcast_add_fusion.2
  251.7 1.2 bitcast_add_fusion.2
  252.9 1.2 bitcast_add_fusion.2
  254.1 1.2 bitcast_add_fusion.2
  255.3 1.2 bitcast_add_fusion.2
  256.5 1.2 bitcast_add_fusion.2
  257.7 1.2 bitcast_add_fusion.2
  263.7 1.2 bitcast_add_fusion.2
  264.9 1.2 bitcast_add_fusion.2
  266.0 1.2 bitcast_add_fusion.2
  267.2 1.2 bitcast_add_fusion.2
  268.4 1.2 bitcast_add_fusion.2
  269.6 1.2 bitcast_add_fusion.2
  274.4 1.2 bitcast_add_fusion.2
  279.7 10.6 %all_to_all.18 = bf16[4,128,256]{1,2,0:T(8,128)(2,1)S(1)} all-to-all(bf16[4,128,256]{1,2,0:T(8,128)(2,1)S(1)} %bitcast.29), channel_id=1, replica_groups=mesh['seq'=32,'heads'=4,'dp'=4] {'dp'}, dimensions={0} | all-to-all | bytes 524288 | tf_op jit(solution)/shard_map/all_to_all | solution.py:77
  (37 shorter events, 21.0 us)
Async XLA Ops:
  6.5 49.2 %all-gather.7.cloned.1.call-start = ((), (), s32[]{:S(2)}) async-start(), calls=%async_computation.2 | async-start | bytes 3932160 | tf_op jit(solution)/shard_map/all_gather | solution.py:63
  7.3 124.9 %all-gather.5.cloned.1.call-start = ((), (), s32[]{:S(2)}) async-start(), calls=%async_computation.1 | async-start | bytes 4866048 | tf_op jit(solution)/shard_map/all_gather | solution.py:70
  8.0 234.1 %all-gather.9.cloned.1.call-start = ((), (), s32[]{:S(2)}) async-start(), calls=%async_computation.3 | async-start | bytes 17301504 | tf_op jit(solution)/shard_map/all_gather | solution.py:11
  242.1 37.4 %copy-start = (f32[256]{0:T(256)S(1)}, f32[256]{0:T(256)}, u32[]{:S(2)}) copy-start(f32[256]{0:T(256)} %param.7) | copy-start | bytes 3076
Sparse Core Ops, SparseCore 0:
  9.5 46.2 all-gather.6
  57.9 74.1 all-gather.4
  139.7 102.3 all-gather.8
where the time goes:
time: 299 us; the launch traced here: 298 us
  waiting for transfers between devices  227 us (76%)
  other arithmetic  36.4 us (12%)
  between operations  13.2 us (4%)
  blocking collectives  10.6 us (4%)
  matrix products  7.57 us (3%)
    all_gather x1, waiting for transfers between devices, prefix_2(): gathered = lax.all_gather(part, axis)  101 us
    all_gather x1, waiting for transfers between devices, body(): lax.all_gather(proj_weights, 'seq', axis=1, tiled=True)  76.4 us
    all_gather x1, waiting for transfers between devices, body(): everyone = lax.all_gather(tokens, 'dp', axis=0, tiled=True)  47.7 us
    add x31, other arithmetic, add_pair(): return earlier + later  36.3 us
    all_to_all x1, blocking collectives, body(): return lax.all_to_all(normed, 'dp', split_axis=0, concat_axis=2, tiled=True)  10.6 us
  transfers between devices with their start and end apart: 3, of which 3 were waited for; matrix products, arithmetic and copies ran while one was open for 0% of the time, Pallas kernels for 0%

commit v1 on v0

--- a/solution.py
+++ b/solution.py
@@ -60,7 +60,22 @@
 
 
 def body(tokens, proj_weights, norm_gain):
-    everyone = lax.all_gather(tokens, "dp", axis=0, tiled=True)
+
+    def clear_inputs(mat):
+        degree = lax.axis_size("dp")
+        piece_next = sorted(((tick, (tick + 1) % degree) for tick in range(degree)))
+        v_now = mat
+        ii = 1
+        slots = [v_now]
+        while ii < degree:
+            v_now = lax.ppermute(v_now, axis_name="dp", perm=piece_next)
+            slots.insert(0, v_now)
+            ii = ii + 1
+        arr_out = jnp.concatenate(slots, axis=0)
+        q_next = lax.axis_index("dp") + 1
+        return jnp.roll(arr_out, q_next * mat.shape[0], axis=0)
+
+    everyone = clear_inputs(tokens)
     seq_count, length, width = everyone.shape
     total_rows = seq_count * length
     per_device = proj_weights.shape[2]

time: 299 us -> 249 us (0.83)
  waiting for transfers between devices: 227 us -> 169 us
  starting transfers between devices: 0.08 us -> 7.1 us
    all_gather x1, waiting for transfers between devices: 76.4 us -> 10.9 us  [body(): lax.all_gather(proj_weights, 'seq', axis=1, tiled=True)]
    ppermute x0 -> x3, waiting for transfers between devices: none -> 55.3 us  [clear_inputs(): v_now = lax.ppermute(v_now, axis_name='dp', perm=piece_next)]
    all_gather x1 -> x0, waiting for transfers between devices: 47.7 us -> none  [body(): everyone = lax.all_gather(tokens, 'dp', axis=0, tiled=True)]
    ppermute x0 -> x3, starting transfers between devices: none -> 7.06 us  [clear_inputs(): v_now = lax.ppermute(v_now, axis_name='dp', perm=piece_next)]
  transfers between devices with their start and end apart: 3 -> 5, of which waited for: 3 -> 5; matrix products, arithmetic and copies ran while one was open for 0% -> 1% of each run, Pallas kernels for 0% -> 0%
where the time goes in v1:
time: 249 us; the launch traced here: 247 us
  waiting for transfers between devices  169 us (68%)
  other arithmetic  36.4 us (15%)
  between operations  13.6 us (5%)
  blocking collectives  10.6 us (4%)
  starting transfers between devices  7.1 us (3%)
  matrix products  6.99 us (3%)
  local copies, waits for them, and re-layouts  3.38 us (1%)
    all_gather x1, waiting for transfers between devices, prefix_2(): gathered = lax.all_gather(part, axis)  102 us
    ppermute x3, waiting for transfers between devices, clear_inputs(): v_now = lax.ppermute(v_now, axis_name='dp', perm=piece_next)  55.3 us
    add x31, other arithmetic, add_pair(): return earlier + later  36.3 us
    all_gather x1, waiting for transfers between devices, body(): lax.all_gather(proj_weights, 'seq', axis=1, tiled=True)  10.9 us
    all_to_all x1, blocking collectives, body(): return lax.all_to_all(normed, 'dp', split_axis=0, concat_axis=2, tiled=True)  10.6 us
    ppermute x3, starting transfers between devices, clear_inputs(): v_now = lax.ppermute(v_now, axis_name='dp', perm=piece_next)  7.06 us
  transfers between devices with their start and end apart: 5, of which 5 were waited for; matrix products, arithmetic and copies ran while one was open for 1% of the time, Pallas kernels for 0%

profile of v1, /device:TPU:481, one launch (start us, length us, event | category | flops | bytes accessed | tf_op | source)
XLA Modules:
  0.0 247.4 jit_solution(1460454438133815926)
XLA Ops:
  7.3 3.2 %collective-permute-start = (bf16[1,128,3072]{2,1,0:T(8,128)(2,1)}, bf16[1,128,3072]{2,1,0:T(8,128)(2,1)S(1)}, u32[]{:S(2)}, u32[]{:S(2)}) collective-permute-start(bf16[1,128,3072]{2,1,0:T(8,128)(2,1)} %param.5), channel_id=1, source_target_pairs={{0,1},{1,2},{2,3},{3,0},{4,5},{5,6},{6,7},{7,4},{8,9},{9,10},{10,1... | collective-permute-start | bytes 2359304 | tf_op jit(solution)/shard_map/ppermute | solution.py:71
  10.5 18.7 %collective-permute-done = bf16[1,128,3072]{2,1,0:T(8,128)(2,1)S(1)} collective-permute-done((bf16[1,128,3072]{2,1,0:T(8,128)(2,1)}, bf16[1,128,3072]{2,1,0:T(8,128)(2,1)S(1)}, u32[]{:S(2)}, u32[]{:S(2)}) %collective-permute-start) | collective-permute-done | bytes 786464 | tf_op jit(solution)/shard_map/ppermute | solution.py:71
  29.2 1.9 collective-permute-start.1
  31.1 18.7 %collective-permute-done.1 = bf16[1,128,3072]{2,1,0:T(8,128)(2,1)S(1)} collective-permute-done((bf16[1,128,3072]{2,1,0:T(8,128)(2,1)S(1)}, bf16[1,128,3072]{2,1,0:T(8,128)(2,1)S(1)}, u32[]{:S(2)}, u32[]{:S(2)}) %collective-permute-start.1) | collective-permute-done | bytes 786464 | tf_op jit(solution)/shard_map/ppermute | solution.py:71
  49.8 1.9 collective-permute-start.2
  51.8 17.9 %collective-permute-done.2 = bf16[1,128,3072]{2,1,0:T(8,128)(2,1)S(1)} collective-permute-done((bf16[1,128,3072]{2,1,0:T(8,128)(2,1)S(1)}, bf16[1,128,3072]{2,1,0:T(8,128)(2,1)S(1)}, u32[]{:S(2)}, u32[]{:S(2)}) %collective-permute-start.2) | collective-permute-done | bytes 786464 | tf_op jit(solution)/shard_map/ppermute | solution.py:71
  69.9 1.2 constant_dynamic-update-slice_fusion.4
  71.5 10.9 %all-gather.4.cloned.1.call-done = bf16[3,3072,256]{2,1,0:T(8,128)(2,1)} async-done(((bf16[3,96,256]{2,1,0:T(8,128)(2,1)}), bf16[3,3072,256]{2,1,0:T(8,128)(2,1)}) %all-gather.4.cloned.1.call-update) | async-done | bytes 4718608 | tf_op jit(solution)/shard_map/all_gather | solution.py:85
  82.4 4.9 %convolution_bitcast_fusion = f32[3,512,256]{2,1,0:T(8,128)S(1)} fusion(bf16[512,3072,1]{1,0,2:T(8,128)(2,1)S(1)} %bitcast.21, bf16[3,3072,256]{2,1,0:T(8,128)(2,1)} %all-gather.4.cloned.1.call-done), kind=kOutput, calls=%fused_computation.1 | convolution fusion | flops 2415919104 | bytes 9437184 | tf_op jit(solution)/shard_map/nd,jdc->jnc/dot_general | solution.py:27
  89.9 101.7 %all-gather.6.cloned.1.call-done = f32[128,2,128,128]{3,2,1,0:T(8,128)} async-done(((f32[4,2,128,128]{3,2,1,0:T(8,128)}), f32[128,2,128,128]{3,2,1,0:T(8,128)}) %all-gather.6.cloned.1.call-update) | async-done | bytes 16777232 | tf_op jit(solution)/shard_map/all_gather | solution.py:11
  191.6 37.0 %while.10 = (s32[]{:T(128)}, f32[4,2,128,128]{3,2,1,0:T(8,128)S(1)}, s32[]{:T(128)}, f32[32,4,2,128,128]{4,3,2,1,0:T(8,128)}, s32[]{:T(128)}, /*index=5*/s32[]{:T(128)}, s32[]{:T(128)}) while((s32[]{:T(128)}, f32[4,2,128,128]{3,2,1,0:T(8,128)S(1)}, s32[]{:T(128)}, f32[32,4,2,128,128]{4,3,2,1,0:T(8,128)}, s32[]{:T(128)}, /*index=5*/s32[]{:T(128)}, ...), condition=%wide.region_1.2_spmd, body=%wide.region_0.1_spmd.sunk | while | flops 131077 | bytes 1572987 | solution.py:17
  191.6 1.2 bitcast_add_fusion.2
  192.8 1.2 bitcast_add_fusion.2
  194.0 1.2 bitcast_add_fusion.2
  195.2 1.2 bitcast_add_fusion.2
  196.4 1.2 bitcast_add_fusion.2
  197.6 1.2 bitcast_add_fusion.2
  202.4 1.2 bitcast_add_fusion.2
  203.6 1.2 bitcast_add_fusion.2
  204.8 1.2 bitcast_add_fusion.2
  206.0 1.2 bitcast_add_fusion.2
  207.2 1.2 bitcast_add_fusion.2
  208.3 1.2 bitcast_add_fusion.2
  229.1 10.6 %all_to_all.18 = bf16[4,128,256]{1,2,0:T(8,128)(2,1)S(1)} all-to-all(bf16[4,128,256]{1,2,0:T(8,128)(2,1)S(1)} %bitcast.22), channel_id=1, replica_groups=mesh['seq'=32,'heads'=4,'dp'=4] {'dp'}, dimensions={0} | all-to-all | bytes 524288 | tf_op jit(solution)/shard_map/all_to_all | solution.py:92
  (48 shorter events, 27.4 us)
Async XLA Ops:
  6.5 64.7 %copy-start = (bf16[1,128,3072]{2,1,0:T(8,128)(2,1)S(1)}, bf16[1,128,3072]{2,1,0:T(8,128)(2,1)}, u32[]{:S(2)}) copy-start(bf16[1,128,3072]{2,1,0:T(8,128)(2,1)} %param.5) | copy-start | bytes 2359300
  6.5 75.9 %all-gather.4.cloned.1.call-start = ((), (), s32[]{:S(2)}) async-start(), calls=%async_computation.1 | async-start | bytes 4866048 | tf_op jit(solution)/shard_map/all_gather | solution.py:85
  7.3 184.3 %all-gather.6.cloned.1.call-start = ((), (), s32[]{:S(2)}) async-start(), calls=%async_computation.2 | async-start | bytes 17301504 | tf_op jit(solution)/shard_map/all_gather | solution.py:11
  7.3 21.9 %collective-permute-start = (bf16[1,128,3072]{2,1,0:T(8,128)(2,1)}, bf16[1,128,3072]{2,1,0:T(8,128)(2,1)S(1)}, u32[]{:S(2)}, u32[]{:S(2)}) collective-permute-start(bf16[1,128,3072]{2,1,0:T(8,128)(2,1)} %param.5), channel_id=1, source_target_pairs={{0,1},{1,2},{2,3},{3,0},{4,5},{5,6},{6,7},{7,4},{8,9},{9,10},{10,1... | collective-permute-start | bytes 2359304 | tf_op jit(solution)/shard_map/ppermute | solution.py:71
  29.2 20.7 %collective-permute-start.1 = (bf16[1,128,3072]{2,1,0:T(8,128)(2,1)S(1)}, bf16[1,128,3072]{2,1,0:T(8,128)(2,1)S(1)}, u32[]{:S(2)}, u32[]{:S(2)}) collective-permute-start(bf16[1,128,3072]{2,1,0:T(8,128)(2,1)S(1)} %collective-permute-done), channel_id=1, source_target_pairs={{0,1},{1,2},{2,3},{3,0},{4,5},{5,6},{6,7},{7,4},{8,9},{9,10},{10,1... | collective-permute-start | bytes 2359304 | tf_op jit(solution)/shard_map/ppermute | solution.py:71
  49.8 19.8 %collective-permute-start.2 = (bf16[1,128,3072]{2,1,0:T(8,128)(2,1)S(1)}, bf16[1,128,3072]{2,1,0:T(8,128)(2,1)S(1)}, u32[]{:S(2)}, u32[]{:S(2)}) collective-permute-start(bf16[1,128,3072]{2,1,0:T(8,128)(2,1)S(1)} %collective-permute-done.1), channel_id=1, source_target_pairs={{0,1},{1,2},{2,3},{3,0},{4,5},{5,6},{6,7},{7,4},{8,9},{9,10},{10,1... | collective-permute-start | bytes 2359304 | tf_op jit(solution)/shard_map/ppermute | solution.py:71
  89.9 139.1 %copy-start.1 = (f32[256]{0:T(256)S(1)}, f32[256]{0:T(256)}, u32[]{:S(2)}) copy-start(f32[256]{0:T(256)} %param.7) | copy-start | bytes 3076
Sparse Core Ops, SparseCore 0:
  9.5 72.8 all-gather.3
  89.1 102.4 all-gather.5
